TPU v7x, 32 devices: a whole 2x2x4 slice. The times are simulated.
32 devices in a mesh: dp: 4 (over y, core), mp: 8 (over z, x).
Axes of the slice: x: 2, y: 2, z: 4, core: 2. Of those that a mesh axis runs over, the one named last changes fastest.
Arguments:
- tokens: bfloat16 [768, 8192], P('dp', 'mp'), may hold values from -6 to 6
- out_grad: bfloat16 [768, 8192], P('dp', 'mp'), may hold values from -6 to 6
- w_gate: bfloat16 [8, 96, 128, 128], P('mp'), may hold values from -0.125 to 0.125
- w_up: bfloat16 [8, 96, 128, 128], P('mp'), may hold values from -0.125 to 0.125
- w_down: bfloat16 [8, 96, 128, 128], P('mp'), may hold values from -0.125 to 0.125
- gu_rows: int32 [8, 96], P('mp'), may hold values from 0 to 63, as said below
- gu_cols: int32 [8, 96], P('mp'), may hold values from 0 to 6
- gu_count: int32 [8], P('mp'), may hold values from 24 to 96, as said below
- dn_rows: int32 [8, 96], P('mp'), may hold values from 0 to 6, as said below
- dn_cols: int32 [8, 96], P('mp'), may hold values from 0 to 63
- dn_count: int32 [8], P('mp'), may hold values from 24 to 96, as said below
Outputs:
- ffn_out: bfloat16 [768, 8192], P('dp', 'mp')
- input_grad: bfloat16 [768, 8192], P('dp', 'mp')
- gate_step: float32 [8, 96, 128, 128], P('mp', 'dp')
- up_step: float32 [8, 96, 128, 128], P('mp', 'dp')
- down_step: float32 [8, 96, 128, 128], P('mp', 'dp')
Inputs may be any that keep to these rules, and one draw needn't show every extreme that they name: Pairs (gu_rows, gu_cols) are distinct within one mp index, slots that are not live included. `gu_count`: some mp index has all 96 slots live. Pairs (dn_rows, dn_cols) are distinct within one mp index, slots that are not live included. `dn_count`: some mp index has all 96 slots live.
All inputs are finite; a program needn't handle non-finite values.
Results may differ from a plain program's by a relative error of at most 0.012.
Values may be sent and summed in bfloat16 or wider, within the bound.
A program may use at most 128 MiB of HBM per device.

v0:
```python
import math

import jax
import jax.numpy as jnp
from jax import lax
from jax.sharding import PartitionSpec as P

HID_DEV = 896


decay_coef = 8.0


def selector(index, length, live):
    return (index[:, None] == jnp.arange(length)[None, :]).astype(jnp.float32) * live[:, None]


def collect(tiles, table):
    return jnp.einsum(
        "tsn,sc->tcn",
        tiles,
        table,
        precision=lax.Precision.HIGH,
        preferred_element_type=jnp.float32,
    )


def tile_grad(left, right):
    return jnp.einsum("tsk,tsn->skn", left, right, preferred_element_type=jnp.float32)


def finish(summed, weights, live, scale_root):
    share = summed.shape[1]
    start = lax.axis_index("dp") * share
    own_w = lax.dynamic_slice_in_dim(weights, start, share, 0).astype(jnp.float32)
    own_live = lax.dynamic_slice_in_dim(live, start, share, 0)
    return ((summed[0] * scale_root + decay_coef * own_w) * own_live[:, None, None])[None]


def local(
    tokens, out_grad, w_gate, w_up, w_down, gu_rows, gu_cols, gu_count, dn_rows, dn_cols, dn_count
):
    block = w_gate.shape[2]
    slots = w_gate.shape[1]
    hblocks = HID_DEV // block
    wg = w_gate[0]
    wu = w_up[0]
    wd = w_down[0]
    features = lax.all_gather(tokens, "mp", axis=1, tiled=True)
    ntok = features.shape[0]
    width = features.shape[1]
    dblocks = width // block
    scale_root = 1.0 / math.sqrt(ntok * lax.axis_size("dp"))
    slot_ids = jnp.arange(slots)
    live = (slot_ids < gu_count[0]).astype(jnp.float32)
    dlive = (slot_ids < dn_count[0]).astype(jnp.float32)
    gate_place = selector(gu_cols[0], hblocks, live)
    gate_back = selector(gu_rows[0], dblocks, live)
    down_place = selector(dn_cols[0], dblocks, dlive)
    down_back = selector(dn_rows[0], hblocks, dlive)
    x_tiles = jnp.take(features.reshape(ntok, dblocks, block), gu_rows[0], axis=1)
    gate_tiles = jnp.einsum("tsk,skn->tsn", x_tiles, wg, preferred_element_type=jnp.float32)
    up_tiles = jnp.einsum("tsk,skn->tsn", x_tiles, wu, preferred_element_type=jnp.float32)
    gate = collect(gate_tiles, gate_place)
    up = collect(up_tiles, gate_place)
    sig = jax.nn.sigmoid(gate)
    act = gate * sig
    hidden = (act * up).astype(jnp.bfloat16)
    h_tiles = jnp.take(hidden, dn_rows[0], axis=1)
    out_tiles = jnp.einsum("tsk,skn->tsn", h_tiles, wd, preferred_element_type=jnp.float32)
    out_part = collect(out_tiles, down_place).reshape(ntok, width)
    ffn_out = lax.psum_scatter(out_part.astype(jnp.bfloat16), "mp", scatter_dimension=1, tiled=True)
    cotangent = lax.all_gather(out_grad, "mp", axis=1, tiled=True)
    dy_tiles = jnp.take(cotangent.reshape(ntok, dblocks, block), dn_cols[0], axis=1)
    dh_tiles = jnp.einsum("tsn,skn->tsk", dy_tiles, wd, preferred_element_type=jnp.float32)
    dhid = collect(dh_tiles, down_back)
    down_grad = tile_grad(h_tiles, dy_tiles)
    d_gate = (dhid * up * sig * (1.0 + gate * (1.0 - sig))).astype(jnp.bfloat16)
    d_up = (dhid * act).astype(jnp.bfloat16)
    dg_tiles = jnp.take(d_gate, gu_cols[0], axis=1)
    du_tiles = jnp.take(d_up, gu_cols[0], axis=1)
    gate_grad = tile_grad(x_tiles, dg_tiles)
    up_grad = tile_grad(x_tiles, du_tiles)
    back_tiles = jnp.einsum("tsn,skn->tsk", dg_tiles, wg, preferred_element_type=jnp.float32)
    back_tiles = back_tiles + jnp.einsum(
        "tsn,skn->tsk", du_tiles, wu, preferred_element_type=jnp.float32
    )
    in_part = collect(back_tiles, gate_back).reshape(ntok, width)
    input_grad = lax.psum_scatter(
        in_part.astype(jnp.bfloat16), "mp", scatter_dimension=1, tiled=True
    )
    gate_summed, up_summed, down_summed = (
        lax.psum_scatter(
            gate_grad[None].astype(jnp.bfloat16), "dp", scatter_dimension=1, tiled=True
        ).astype(jnp.float32),
        lax.psum_scatter(
            up_grad[None].astype(jnp.bfloat16), "dp", scatter_dimension=1, tiled=True
        ).astype(jnp.float32),
        lax.psum_scatter(
            down_grad[None].astype(jnp.bfloat16), "dp", scatter_dimension=1, tiled=True
        ).astype(jnp.float32),
    )
    gate_step = finish(gate_summed, wg, live, scale_root)
    up_step = finish(up_summed, wu, live, scale_root)
    down_step = finish(down_summed, wd, dlive, scale_root)
    return (ffn_out, input_grad, gate_step, up_step, down_step)


def solution(mesh):
    in_specs = (
        P("dp", "mp"),
        P("dp", "mp"),
        P("mp", None, None, None),
        P("mp", None, None, None),
        P("mp", None, None, None),
        P("mp", None),
        P("mp", None),
        P("mp"),
        P("mp", None),
        P("mp", None),
        P("mp"),
    )
    out_specs = (
        P("dp", "mp"),
        P("dp", "mp"),
        P("mp", "dp", None, None),
        P("mp", "dp", None, None),
        P("mp", "dp", None, None),
    )
    return jax.shard_map(local, mesh=mesh, in_specs=in_specs, out_specs=out_specs, check_vma=False)
```

profile of v0, /device:TPU:0, one launch (start us, length us, event | category | flops | bytes accessed | tf_op | source)
XLA Modules:
  0.0 460.3 jit_solution(3682430924706006872)
XLA Ops:
  13.4 60.0 %all-gather.3.cloned.1.call-done = bf16[192,8192]{1,0:T(8,128)(2,1)} async-done(((bf16[192,1024]{1,0:T(8,128)(2,1)}), bf16[192,8192]{1,0:T(8,128)(2,1)}) %all-gather.3.cloned.1.call-update) | async-done | bytes 3145744 | tf_op jit(solution)/shard_map/all_gather | solution.py:49
  79.6 5.1 %fusion.34 = f32[192,96,128]{2,0,1:T(8,128)S(1)} fusion(bf16[1,96,128,128]{3,2,1,0:T(8,128)(2,1)} %param.18, bf16[96,192,128]{2,1,0:T(8,128)(2,1)} %gather_fusion, pred[96]{0:T(512)(128)(4,1)S(1)} %get-tuple-element.17), kind=kOutput, calls=%fused_computation.43 | convolution fusion | flops 606339072 | bytes 17301600 | tf_op jit(solution)/shard_map/tsk,skn->tsn/dot_general | solution.py:63
  84.7 8.1 %fusion.6 = f32[7,192,128]{2,0,1:T(8,128)} fusion(f32[192,96,128]{2,0,1:T(8,128)S(1)} %fusion.34, f32[96]{0:T(128)S(1)} %compare_convert_fusion, s32[96]{0:T(128)S(1)} %bitcast.178), kind=kOutput, calls=%fused_computation.11 | convolution fusion | flops 99091776 | bytes 10126080 | tf_op jit(solution)/shard_map/tsn,sc->tcn/dot_general | solution.py:19
  94.3 8.4 %fusion.8 = f32[7,192,128]{2,0,1:T(8,128)} fusion(f32[192,96,128]{2,0,1:T(8,128)S(1)} %fusion.31, f32[96]{0:T(128)S(1)} %compare_convert_fusion, s32[96]{0:T(128)S(1)} %bitcast.179), kind=kOutput, calls=%fused_computation.13 | convolution fusion | flops 99091776 | bytes 10126080 | tf_op jit(solution)/shard_map/tsn,sc->tcn/dot_general | solution.py:19
  102.7 32.1 %all-gather.5.cloned.1.call-done = bf16[192,8192]{1,0:T(8,128)(2,1)} async-done(((bf16[192,1024]{1,0:T(8,128)(2,1)}), bf16[192,8192]{1,0:T(8,128)(2,1)}) %all-gather.5.cloned.1.call-update) | async-done | bytes 3145744 | tf_op jit(solution)/shard_map/all_gather | solution.py:73
  137.6 3.5 gather_fusion.2
  141.0 5.5 %fusion.40 = f32[192,96,128]{2,0,1:T(8,128)S(1)} fusion(bf16[1,96,128,128]{3,2,1,0:T(8,128)(2,1)} %param.19, bf16[96,192,128]{2,1,0:T(8,128)(2,1)} %gather_fusion.2, pred[96]{0:T(512)(128)(4,1)S(1)} %get-tuple-element.15), kind=kOutput, calls=%fused_computation.45 | convolution fusion | flops 606339072 | bytes 17301600 | tf_op jit(solution)/shard_map/tsn,skn->tsk/dot_general | solution.py:75
  146.6 19.1 %fusion.2 = f32[7,192,128]{2,0,1:T(8,128)S(1)} fusion(f32[192,96,128]{2,0,1:T(8,128)S(1)} %fusion.40, f32[96]{0:T(128)S(1)} %compare_convert_fusion.1, s32[96]{0:T(128)S(1)} %bitcast.180), kind=kOutput, calls=%fused_computation.7 | convolution fusion | flops 99091776 | bytes 10126080 | tf_op jit(solution)/shard_map/tsn,sc->tcn/dot_general | solution.py:19
  166.2 3.5 gather_fusion.1
  169.8 7.7 %convert_bitcast_fusion = bf16[1,96,128,128]{3,2,1,0:T(8,128)(2,1)} fusion(bf16[96,192,128]{2,1,0:T(8,128)(2,1)} %gather_fusion.1, pred[96]{0:T(512)(128)(4,1)S(1)} %get-tuple-element.16, bf16[96,192,128]{2,1,0:T(8,128)(2,1)} %gather_fusion.2, pred[96]{0:T(512)(128)(4,1)S(1)} %get-tuple-element.15), kind=kOutput, calls=%fused_computation.56 | convolution fusion | flops 610271232 | bytes 12583104 | tf_op jit(solution)/shard_map/tsk,tsn->skn/dot_general | solution.py:29
  181.0 8.7 %convert_bitcast_fusion.2 = bf16[1,96,128,128]{3,2,1,0:T(8,128)(2,1)} fusion(bf16[96,192,128]{2,1,0:T(8,128)(2,1)} %gather_fusion.3, pred[96]{0:T(512)(128)(4,1)S(1)} %get-tuple-element.14, bf16[96,192,128]{2,1,0:T(8,128)(2,1)} %gather_fusion, pred[96]{0:T(512)(128)(4,1)S(1)} %get-tuple-element.17), kind=kOutput, calls=%fused_computation.58 | convolution fusion | flops 610271232 | bytes 12583104 | tf_op jit(solution)/shard_map/tsk,tsn->skn/dot_general | solution.py:29
  189.8 3.5 gather_fusion.4
  193.3 8.1 %convert_bitcast_fusion.1 = bf16[1,96,128,128]{3,2,1,0:T(8,128)(2,1)} fusion(bf16[96,192,128]{2,1,0:T(8,128)(2,1)} %gather_fusion.4, pred[96]{0:T(512)(128)(4,1)S(1)} %get-tuple-element.14, bf16[96,192,128]{2,1,0:T(8,128)(2,1)} %gather_fusion, pred[96]{0:T(512)(128)(4,1)S(1)} %get-tuple-element.17), kind=kOutput, calls=%fused_computation.57 | convolution fusion | flops 610271232 | bytes 12583104 | tf_op jit(solution)/shard_map/tsk,tsn->skn/dot_general | solution.py:29
  203.3 4.4 fusion.12
  207.8 9.2 %add_bitcast_fusion = f32[192,96,128]{2,0,1:T(8,128)} fusion(f32[96,192,128]{2,1,0:T(8,128)S(1)} %fusion.12, bf16[1,96,128,128]{3,2,1,0:T(8,128)(2,1)} %param.17, bf16[96,192,128]{2,1,0:T(8,128)(2,1)} %gather_fusion.3, pred[96]{0:T(512)(128)(4,1)S(1)} %get-tuple-element.14), kind=kOutput, calls=%fused_computation.15 | convolution fusion | flops 608698368 | bytes 26738784 | tf_op jit(solution)/shard_map/tsn,skn->tsk/dot_general | solution.py:84
  217.0 12.1 %fusion.66 = bf16[64,192,128]{2,0,1:T(8,128)(2,1)S(1)} fusion(f32[192,96,128]{2,0,1:T(8,128)} %add_bitcast_fusion, f32[96]{0:T(128)S(1)} %compare_convert_fusion, s32[96]{0:T(128)S(1)} %bitcast.181), kind=kOutput, calls=%fused_computation.60 | convolution fusion | flops 907554816 | bytes 12583680 | tf_op jit(solution)/shard_map/tsn,sc->tcn/dot_general | solution.py:19
  229.1 4.7 %copy.74 = bf16[24,8,64,128]{3,1,2,0:T(8,128)(2,1)} copy(bf16[24,8,64,128]{3,2,1,0:T(8,128)(2,1)S(1)} %bitcast.176) | data formatting | bytes 6291456
  233.9 3.8 fusion.37
  237.7 12.4 %fusion.63 = bf16[64,192,128]{2,0,1:T(8,128)(2,1)S(1)} fusion(f32[192,96,128]{2,0,1:T(8,128)S(1)} %fusion.37, f32[96]{0:T(128)S(1)} %compare_convert_fusion.1, s32[96]{0:T(128)S(1)} %bitcast.182), kind=kOutput, calls=%fused_computation.59 | convolution fusion | flops 907554816 | bytes 12583680 | tf_op jit(solution)/shard_map/tsn,sc->tcn/dot_general | solution.py:19
  250.1 4.5 copy.75
  257.4 37.8 %reduce-scatter.12.cloned.1.call-done = bf16[1,24,128,128]{3,2,1,0:T(8,128)(2,1)} async-done(((bf16[1,96,128,128]{3,2,1,0:T(8,128)(2,1)}), bf16[1,24,128,128]{3,2,1,0:T(8,128)(2,1)}) %reduce-scatter.12.cloned.1.call-update) | async-done | bytes 786448 | tf_op jit(solution)/shard_map/reduce_scatter | solution.py:96
  295.1 4.2 add_multiply_fusion.1
  299.3 75.3 %reduce-scatter.8.cloned.1.call-done = bf16[192,1024]{1,0:T(8,128)(2,1)} async-done(((bf16[192,8192]{1,0:T(8,128)(2,1)}), bf16[192,1024]{1,0:T(8,128)(2,1)}) %reduce-scatter.8.cloned.1.call-update) | async-done | bytes 393232 | tf_op jit(solution)/shard_map/reduce_scatter | solution.py:89
  374.6 78.6 %reduce-scatter.6.cloned.1.call-done = bf16[192,1024]{1,0:T(8,128)(2,1)} async-done(((bf16[192,8192]{1,0:T(8,128)(2,1)}), bf16[192,1024]{1,0:T(8,128)(2,1)}) %reduce-scatter.6.cloned.1.call-update) | async-done | bytes 393232 | tf_op jit(solution)/shard_map/reduce_scatter | solution.py:72
  (56 shorter events, 24.1 us)
Async XLA Ops:
  7.2 66.3 %all-gather.3.cloned.1.call-start = ((), (), s32[]{:S(2)}) async-start(), calls=%async_computation.5 | async-start | bytes 3538944 | tf_op jit(solution)/shard_map/all_gather | solution.py:49
  7.9 126.9 %all-gather.5.cloned.1.call-start = ((), (), s32[]{:S(2)}) async-start(), calls=%async_computation.7 | async-start | bytes 3538944 | tf_op jit(solution)/shard_map/all_gather | solution.py:73
  8.6 246.1 %reduce-scatter.14.cloned.1.call-start = ((), (), s32[]{:S(2)}) async-start(), calls=%async_computation.11 | async-start | bytes 3932160 | tf_op jit(solution)/shard_map/reduce_scatter | solution.py:99
  79.6 5.1 %copy-start.6 = (s32[1,96]{1,0:T(1,128)S(1)}, s32[1,96]{1,0:T(1,128)}, u32[]{:S(2)}) copy-start(s32[1,96]{1,0:T(1,128)} %param.21) | copy-start | bytes 1156
  84.7 8.1 %copy-start = (bf16[96,192,128]{2,1,0:T(8,128)(2,1)S(1)}, bf16[96,192,128]{2,1,0:T(8,128)(2,1)}, u32[]{:S(2)}) copy-start(bf16[96,192,128]{2,1,0:T(8,128)(2,1)} %gather_fusion) | copy-start | bytes 14155780
  84.7 8.1 %copy-start.3 = (bf16[1,96,128,128]{3,2,1,0:T(8,128)(2,1)S(1)}, bf16[1,96,128,128]{3,2,1,0:T(8,128)(2,1)}, u32[]{:S(2)}) copy-start(bf16[1,96,128,128]{3,2,1,0:T(8,128)(2,1)} %param.17) | copy-start | bytes 9437188
  141.0 5.5 %copy-start.7 = (s32[1,96]{1,0:T(1,128)S(1)}, s32[1,96]{1,0:T(1,128)}, u32[]{:S(2)}) copy-start(s32[1,96]{1,0:T(1,128)} %param.23) | copy-start | bytes 1156
  146.6 19.1 %copy-start.4 = (f32[7,192,128]{2,0,1:T(8,128)S(1)}, f32[7,192,128]{2,0,1:T(8,128)}, u32[]{:S(2)}) copy-start(f32[7,192,128]{2,0,1:T(8,128)} %fusion.6) | copy-start | bytes 2064388
  146.6 19.1 %copy-start.5 = (f32[7,192,128]{2,0,1:T(8,128)S(1)}, f32[7,192,128]{2,0,1:T(8,128)}, u32[]{:S(2)}) copy-start(f32[7,192,128]{2,0,1:T(8,128)} %fusion.8) | copy-start | bytes 2064388
  177.5 79.9 %reduce-scatter.10.cloned.1.call-start = ((), (), s32[]{:S(2)}) async-start(), calls=%async_computation.9 | async-start | bytes 3932160 | tf_op jit(solution)/shard_map/reduce_scatter | solution.py:93
  189.7 105.4 %reduce-scatter.12.cloned.1.call-start = ((), (), s32[]{:S(2)}) async-start(), calls=%async_computation.10 | async-start | bytes 3932160 | tf_op jit(solution)/shard_map/reduce_scatter | solution.py:96
  201.4 1.9 copy-start.2
  201.4 173.2 %reduce-scatter.8.cloned.1.call-start = ((), (), s32[]{:S(2)}) async-start(), calls=%async_computation.8 | async-start | bytes 3538944 | tf_op jit(solution)/shard_map/reduce_scatter | solution.py:89
  207.7 9.3 %copy-start.8 = (s32[1,96]{1,0:T(1,128)S(1)}, s32[1,96]{1,0:T(1,128)}, u32[]{:S(2)}) copy-start(s32[1,96]{1,0:T(1,128)} %param.20) | copy-start | bytes 1156
  229.1 4.8 %copy-start.1 = (bf16[1,96,128,128]{3,2,1,0:T(8,128)(2,1)S(1)}, bf16[1,96,128,128]{3,2,1,0:T(8,128)(2,1)}, u32[]{:S(2)}) copy-start(bf16[1,96,128,128]{3,2,1,0:T(8,128)(2,1)} %param.19) | copy-start | bytes 9437188
  233.8 3.9 copy-start.9
  233.8 219.4 %reduce-scatter.6.cloned.1.call-start = ((), (), s32[]{:S(2)}) async-start(), calls=%async_computation.6 | async-start | bytes 3538944 | tf_op jit(solution)/shard_map/reduce_scatter | solution.py:72
Sparse Core Ops, SparseCore 0:
  10.2 63.1 all-gather.2
  75.6 59.1 all-gather.4
  177.6 36.5 reduce-scatter.13
  216.8 37.9 reduce-scatter.9
  257.2 37.9 reduce-scatter.11
  299.6 74.9 reduce-scatter.7
  379.2 73.9 reduce-scatter.5
where the time goes:
time: 464 us; the launch traced here: 460 us
  waiting for transfers between devices  285 us (61%)
  matrix products  114 us (25%)
  local copies, waits for them, and re-layouts  34.2 us (7%)
  between operations  15.8 us (3%)
  other arithmetic  10.7 us (2%)
    reduce_scatter x1, waiting for transfers between devices, local(): lax.psum_scatter(out_part.astype(jnp.bfloat16), 'mp', scatter_dimension=1...  78.6 us
    reduce_scatter x1, waiting for transfers between devices, local(): lax.psum_scatter(in_part.astype(jnp.bfloat16), 'mp', scatter_dimension=1,...  75.3 us
    all_gather x1, waiting for transfers between devices, local(): features = lax.all_gather(tokens, 'mp', axis=1, tiled=True)  60 us
    dot_general x5, matrix products, collect(): jnp.einsum('tsn,sc->tcn', tiles, table, precision=lax.Precision.HIGH, pre...  60 us
    reduce_scatter x1, waiting for transfers between devices, local(): lax.psum_scatter(up_grad[None].astype(jnp.bfloat16), 'dp', scatter_dimens...  37.8 us
    all_gather x1, waiting for transfers between devices, local(): cotangent = lax.all_gather(out_grad, 'mp', axis=1, tiled=True)  32.1 us
    dot_general x3, matrix products, tile_grad(): jnp.einsum('tsk,tsn->skn', left, right, preferred_element_type=jnp.float32)  24.6 us
    unnamed x22, local copies, waits for them, and re-layouts  11.1 us
  transfers between devices with their start and end apart: 7, of which 5 were waited for; matrix products, arithmetic and copies ran while one was open for 25% of the time, Pallas kernels for 0%

commit v1 on v0

v1 whole, which is shorter than its diff:
```python
import functools
import math

import jax
import jax.numpy as jnp
from jax import lax
from jax.experimental import pallas as pl
from jax.experimental.pallas import tpu as pltpu
from jax.sharding import PartitionSpec as P

HID_DEV = 896
MESH = pl.DeviceIdType.MESH
F32 = jnp.float32
BF16 = jnp.bfloat16

decay_coef = 8.0


def ring_position(index, n):
    half, odd = index // 2, index % 2
    return (1 - odd) * half + odd * (n - 1 - half)


def ring_device(position, n):
    late = position // (n // 2)
    return (1 - late) * (2 * position) + late * (2 * (n - 1 - position) + 1)


def gather_kernel(n, x_ref, dy_ref, xf_ref, dyf_ref, send_sem, recv_sem, own_sem):
    me = lax.axis_index("mp")
    pos = ring_position(me, n)
    half = x_ref.shape[0] // 2
    target = [ring_device((pos + 1) % n, n), ring_device((pos + n - 1) % n, n)]

    barrier = pltpu.get_barrier_semaphore()
    for device in target:
        pl.semaphore_signal(barrier, inc=1, device_id={"mp": device}, device_id_type=MESH)
    pl.semaphore_wait(barrier, 2)

    pairs = ((x_ref, xf_ref), (dy_ref, dyf_ref))
    own = [
        pltpu.make_async_copy(shard, full.at[me], own_sem.at[a])
        for a, (shard, full) in enumerate(pairs)
    ]

    def hop(a, d, s):
        shard, full = pairs[a]
        rows = pl.ds(d * half, half)
        owner = ring_device((pos + (n - s if d == 0 else s)) % n, n)
        src = shard.at[rows] if s == 0 else full.at[owner, rows]
        return pltpu.make_async_remote_copy(
            src_ref=src,
            dst_ref=full.at[owner, rows],
            send_sem=send_sem.at[a, d, s],
            recv_sem=recv_sem.at[a, d, s],
            device_id={"mp": target[d]},
            device_id_type=MESH,
        )

    copies = {}
    for s in range(n - 1):
        for a in range(2):
            for d in range(2):
                if s > 0:
                    copies[a, d, s - 1].wait_recv()
                copies[a, d, s] = hop(a, d, s)
                copies[a, d, s].start()
        if s == 0:
            for copy in own:
                copy.start()
    for a in range(2):
        for d in range(2):
            copies[a, d, n - 2].wait_recv()
    for copy in own:
        copy.wait()
    for copy in copies.values():
        copy.wait_send()


def gather(tokens, out_grad, n):
    full = jax.ShapeDtypeStruct((n,) + tokens.shape, BF16)
    return pl.pallas_call(
        functools.partial(gather_kernel, n),
        out_shape=(full, full),
        in_specs=[pl.BlockSpec(memory_space=pl.ANY)] * 2,
        out_specs=(pl.BlockSpec(memory_space=pl.ANY),) * 2,
        scratch_shapes=[
            pltpu.SemaphoreType.DMA((2, 2, n - 1)),
            pltpu.SemaphoreType.DMA((2, 2, n - 1)),
            pltpu.SemaphoreType.DMA((2,)),
        ],
        compiler_params=pltpu.CompilerParams(collective_id=0, has_side_effects=True),
    )(tokens, out_grad)


GROUP = 4


def dot(left, right, contract):
    return lax.dot_general(left, right, (contract, ((), ())), preferred_element_type=F32)


def compute_kernel(
    rows_ref, cols_ref, count_ref, drows_ref, dcols_ref, dcount_ref,
    x_ref, dy_ref, wg_ref, wu_ref, wd_ref,
    out_ref, in_ref, grad_ref,
    gu_acc, dh_acc, hid, dgu, wide,
):
    blk = wg_ref.shape[-1]
    per = x_ref.shape[2] // blk
    count = count_ref[0]
    dcount = dcount_ref[0]
    steps = (count + GROUP - 1) // GROUP
    dsteps = (dcount + GROUP - 1) // GROUP

    def place(block):
        return block // per, pl.ds(pl.multiple_of((block % per) * blk, blk), blk)

    def tile(ref, block):
        part, lanes = place(block)
        return ref[part, :, lanes]

    def gated(s):
        both = jnp.concatenate([wg_ref[s], wu_ref[s]], axis=1)
        return jnp.where(s < count, both, jnp.zeros_like(both))

    def down(s):
        return jnp.where(s < dcount, wd_ref[s], jnp.zeros_like(wd_ref[s]))

    gu_acc[...] = jnp.zeros_like(gu_acc)
    dh_acc[...] = jnp.zeros_like(dh_acc)

    def forward(i, carry):
        slots = [i * GROUP + j for j in range(GROUP)]
        parts = [dot(tile(x_ref, rows_ref[s]), gated(s), ((1,), (0,))) for s in slots]
        for s, part in zip(slots, parts):
            gu_acc[cols_ref[s]] += part
        return carry

    lax.fori_loop(0, steps, forward, 0)

    def hidden_back(i, carry):
        slots = [i * GROUP + j for j in range(GROUP)]
        parts = [dot(tile(dy_ref, dcols_ref[s]), down(s), ((1,), (1,))) for s in slots]
        for s, part in zip(slots, parts):
            dh_acc[drows_ref[s]] += part
        return carry

    lax.fori_loop(0, dsteps, hidden_back, 0)

    def pointwise(h, carry):
        gate = gu_acc[h, :, :blk]
        up = gu_acc[h, :, blk:]
        dhid = dh_acc[h]
        sig = 1.0 / (1.0 + jnp.exp(-gate))
        act = gate * sig
        hid[h] = (act * up).astype(BF16)
        dgu[h, :, :blk] = (dhid * up * sig * (1.0 + gate * (1.0 - sig))).astype(BF16)
        dgu[h, :, blk:] = (dhid * act).astype(BF16)
        return carry

    lax.fori_loop(0, gu_acc.shape[0], pointwise, 0)

    def clear(p, carry):
        wide[p] = jnp.zeros(wide.shape[1:], F32)
        return carry

    lax.fori_loop(0, wide.shape[0], clear, 0)

    def down_step(i, carry):
        slots = [i * GROUP + j for j in range(GROUP)]
        hs = [hid[drows_ref[s]] for s in slots]
        parts = [dot(h, down(s), ((1,), (0,))) for s, h in zip(slots, hs)]
        for s, h in zip(slots, hs):
            grad_ref[2, s] = dot(h, tile(dy_ref, dcols_ref[s]), ((0,), (0,))).astype(BF16)
        for s, part in zip(slots, parts):
            at, lanes = place(dcols_ref[s])
            wide[at, :, lanes] += part
        return carry

    lax.fori_loop(0, dsteps, down_step, 0)

    def flush(ref):
        def body(p, carry):
            ref[p] = wide[p].astype(BF16)
            wide[p] = jnp.zeros(wide.shape[1:], F32)
            return carry
        lax.fori_loop(0, wide.shape[0], body, 0)

    flush(out_ref)

    def gate_step(i, carry):
        slots = [i * GROUP + j for j in range(GROUP)]
        gs = [dgu[cols_ref[s]] for s in slots]
        parts = [dot(g, gated(s), ((1,), (1,))) for s, g in zip(slots, gs)]
        for s, g in zip(slots, gs):
            both = dot(tile(x_ref, rows_ref[s]), g, ((0,), (0,))).astype(BF16)
            grad_ref[0, s] = both[:, :blk]
            grad_ref[1, s] = both[:, blk:]
        for s, part in zip(slots, parts):
            at, lanes = place(rows_ref[s])
            wide[at, :, lanes] += part
        return carry

    lax.fori_loop(0, steps, gate_step, 0)
    flush(in_ref)

    def dead(s, carry):
        @pl.when(s >= count)
        def _():
            grad_ref[0, s] = jnp.zeros((blk, blk), BF16)
            grad_ref[1, s] = jnp.zeros((blk, blk), BF16)

        @pl.when(s >= dcount)
        def _():
            grad_ref[2, s] = jnp.zeros((blk, blk), BF16)

        return carry

    lax.fori_loop(0, grad_ref.shape[1], dead, 0)


def compute(xf, dyf, wg, wu, wd, rows, cols, count, drows, dcols, dcount):
    n, ntok, width = xf.shape
    slots, blk, _ = wg.shape
    hblocks = HID_DEV // blk
    full = jax.ShapeDtypeStruct(xf.shape, BF16)
    return pl.pallas_call(
        compute_kernel,
        out_shape=(full, full, jax.ShapeDtypeStruct((3, slots, blk, blk), BF16)),
        in_specs=[pl.BlockSpec(memory_space=pltpu.SMEM)] * 6
        + [pl.BlockSpec(memory_space=pltpu.VMEM)] * 5,
        out_specs=(pl.BlockSpec(memory_space=pltpu.VMEM),) * 3,
        scratch_shapes=[
            pltpu.VMEM((hblocks, ntok, 2 * blk), F32),
            pltpu.VMEM((hblocks, ntok, blk), F32),
            pltpu.VMEM((hblocks, ntok, blk), BF16),
            pltpu.VMEM((hblocks, ntok, 2 * blk), BF16),
            pltpu.VMEM((n, ntok, width), F32),
        ],
        compiler_params=pltpu.CompilerParams(vmem_limit_bytes=56 << 20),
    )(rows, cols, count, drows, dcols, dcount, xf, dyf, wg, wu, wd)


def scatter_kernel(
    n, nd, op_ref, ip_ref, grad_ref, out_ref, in_ref, sum_ref,
    ring, pair, far, ring_send, ring_recv, pair_send, pair_recv, far_send, far_recv,
):
    me = lax.axis_index("mp")
    pos = ring_position(me, n)
    half = out_ref.shape[0] // 2
    target = [ring_device((pos + 1) % n, n), ring_device((pos + n - 1) % n, n)]
    dp = lax.axis_index("dp")
    ny = nd // 2
    y, core = dp // 2, dp % 2
    partner = 2 * y + (1 - core)
    ahead = 2 * ((y + 1) % ny) + core
    behind = 2 * ((y + ny - 1) % ny) + core

    barrier = pltpu.get_barrier_semaphore()
    greet = [{"mp": target[0]}, {"mp": target[1]}, {"dp": partner}, {"dp": ahead}]
    if ny > 2:
        greet.append({"dp": behind})
    for device in greet:
        pl.semaphore_signal(barrier, inc=1, device_id=device, device_id_type=MESH)
    pl.semaphore_wait(barrier, len(greet))

    parts = (op_ref, ip_ref)
    results = (out_ref, in_ref)
    started = []

    def remote(src, dst, send, recv, device):
        copy = pltpu.make_async_remote_copy(
            src_ref=src, dst_ref=dst, send_sem=send, recv_sem=recv,
            device_id=device, device_id_type=MESH,
        )
        copy.start()
        started.append(copy)
        return copy

    def chunk(d, s):
        return ring_device((pos + (2 * n - 1 - s if d == 0 else 1 + s)) % n, n)

    def ring_hop(a, d, s):
        rows = pl.ds(d * half, half)
        src = parts[a].at[chunk(d, 0), rows] if s == 0 else ring.at[a, d, s - 1]
        return remote(
            src, ring.at[a, d, s], ring_send.at[a, d, s], ring_recv.at[a, d, s], {"mp": target[d]}
        )

    def ring_add(a, d, s):
        own = chunk(d, s + 1)
        step = 32

        def body(i, carry):
            r = pl.multiple_of(i * step, step)
            mine = parts[a][own, pl.ds(d * half + r, step), :].astype(F32)
            total = (ring[a, d, s, pl.ds(r, step), :].astype(F32) + mine).astype(BF16)
            if s < n - 2:
                ring[a, d, s, pl.ds(r, step), :] = total
            else:
                results[a][pl.ds(d * half + r, step), :] = total
            return carry

        lax.fori_loop(0, half // step, body, 0)

    def group(t):
        return (y + 2 * ny - 1 - t) % ny

    hops = {}
    for d in range(2):
        for a in range(2):
            hops[a, d] = ring_hop(a, d, 0)
    pairs = {}
    for t in range(ny):
        for k in range(3):
            pairs[k, t] = remote(
                grad_ref.at[k, group(t), 1 - core], pair.at[k, group(t)],
                pair_send.at[k, t], pair_recv.at[k, t], {"dp": partner},
            )
    fars = {}

    def pair_add(k, t):
        pairs[k, t].wait_recv()
        g = group(t)
        if t > 0:
            fars[k, t - 1].wait_recv()

        def body(i, carry):
            total = pair[k, g, i].astype(F32) + grad_ref[k, g, core, i].astype(F32)
            if t > 0:
                total = total + far[k, t - 1, i].astype(F32)
            if t < ny - 1:
                pair[k, g, i] = total.astype(BF16)
            else:
                sum_ref[k, i] = total
            return carry

        lax.fori_loop(0, sum_ref.shape[1], body, 0)
        if t < ny - 1:
            fars[k, t] = remote(
                pair.at[k, g], far.at[k, t], far_send.at[k, t], far_recv.at[k, t], {"dp": ahead}
            )

    for k in range(3):
        pair_add(k, 0)
    for s in range(n - 1):
        for a in range(2):
            for d in range(2):
                hops[a, d].wait_recv()
                ring_add(a, d, s)
                if s < n - 2:
                    hops[a, d] = ring_hop(a, d, s + 1)
    for t in range(1, ny):
        for k in range(3):
            pair_add(k, t)
    for copy in started:
        copy.wait_send()


def scatter(out_part, in_part, grads, nd):
    n, ntok, width = out_part.shape
    _, slots, blk, _ = grads.shape
    share = slots // nd
    ny = nd // 2
    grads = grads.reshape(3, ny, 2, share, blk, blk)
    return pl.pallas_call(
        functools.partial(scatter_kernel, n, nd),
        out_shape=(
            jax.ShapeDtypeStruct((ntok, width), BF16),
            jax.ShapeDtypeStruct((ntok, width), BF16),
            jax.ShapeDtypeStruct((3, share, blk, blk), F32),
        ),
        in_specs=[pl.BlockSpec(memory_space=pltpu.VMEM)] * 3,
        out_specs=(pl.BlockSpec(memory_space=pltpu.VMEM),) * 3,
        scratch_shapes=[
            pltpu.VMEM((2, 2, n - 1, ntok // 2, width), BF16),
            pltpu.VMEM((3, ny, share, blk, blk), BF16),
            pltpu.VMEM((3, max(ny - 1, 1), share, blk, blk), BF16),
            pltpu.SemaphoreType.DMA((2, 2, n - 1)),
            pltpu.SemaphoreType.DMA((2, 2, n - 1)),
            pltpu.SemaphoreType.DMA((3, ny)),
            pltpu.SemaphoreType.DMA((3, ny)),
            pltpu.SemaphoreType.DMA((3, ny)),
            pltpu.SemaphoreType.DMA((3, ny)),
        ],
        compiler_params=pltpu.CompilerParams(
            collective_id=1, has_side_effects=True, vmem_limit_bytes=56 << 20
        ),
    )(out_part, in_part, grads)


def finish(summed, weights, count, scale_root):
    share = summed.shape[0]
    start = lax.axis_index("dp") * share
    own_w = lax.dynamic_slice_in_dim(weights, start, share, 0).astype(F32)
    live = start + jnp.arange(share) < count[0]
    return jnp.where(live[:, None, None], summed * scale_root + decay_coef * own_w, 0.0)[None]


def local(
    tokens, out_grad, w_gate, w_up, w_down, gu_rows, gu_cols, gu_count, dn_rows, dn_cols, dn_count
):
    n = lax.axis_size("mp")
    nd = lax.axis_size("dp")
    wg, wu, wd = w_gate[0], w_up[0], w_down[0]
    scale_root = 1.0 / math.sqrt(tokens.shape[0] * nd)
    xf, dyf = gather(tokens, out_grad, n)
    out_part, in_part, grads = compute(
        xf, dyf, wg, wu, wd, gu_rows[0], gu_cols[0], gu_count, dn_rows[0], dn_cols[0], dn_count
    )
    ffn_out, input_grad, summed = scatter(out_part, in_part, grads, nd)
    gate_step = finish(summed[0], wg, gu_count, scale_root)
    up_step = finish(summed[1], wu, gu_count, scale_root)
    down_step = finish(summed[2], wd, dn_count, scale_root)
    return (ffn_out, input_grad, gate_step, up_step, down_step)


def solution(mesh):
    in_specs = (
        P("dp", "mp"),
        P("dp", "mp"),
        P("mp", None, None, None),
        P("mp", None, None, None),
        P("mp", None, None, None),
        P("mp", None),
        P("mp", None),
        P("mp"),
        P("mp", None),
        P("mp", None),
        P("mp"),
    )
    out_specs = (
        P("dp", "mp"),
        P("dp", "mp"),
        P("mp", "dp", None, None),
        P("mp", "dp", None, None),
        P("mp", "dp", None, None),
    )
    return jax.shard_map(local, mesh=mesh, in_specs=in_specs, out_specs=out_specs, check_vma=False)
```

time: 464 us -> 188 us (0.41)
  waiting for transfers between devices: 285 us -> 0 us
  Pallas kernels: 0 us -> 178 us
  matrix products: 114 us -> 0 us
  local copies, waits for them, and re-layouts: 34.2 us -> 1.5 us
  between operations: 15.8 us -> 1.97 us
  other arithmetic: 10.7 us -> 5.83 us
    reduce_scatter x5 -> x0, waiting for transfers between devices: 192 us -> none  [the longest x1 78.6 us: local(): lax.psum_scatter(out_part.astype(jnp.bfloat16), 'mp', scatter_dimension=1...]
    pallas_call x0 -> x3, Pallas kernels: none -> 178 us  [the longest x1 75.8 us: scatter(): pl.pallas_call(functools.partial(scatter_kernel, n, nd), out_shape=(jax.S...]
    dot_general x14 -> x0, matrix products: 114 us -> none  [the longest x5 60 us: collect(): jnp.einsum('tsn,sc->tcn', tiles, table, precision=lax.Precision.HIGH, pre...]
    all_gather x2 -> x0, waiting for transfers between devices: 92.1 us -> none  [the longest x1 60 us: local(): features = lax.all_gather(tokens, 'mp', axis=1, tiled=True)]
    gather x5 -> x0, local copies, waits for them, and re-layouts: 17.4 us -> none  [the longest x1 3.54 us: local(): h_tiles = jnp.take(hidden, dn_rows[0], axis=1)]
    unnamed x22 -> x6, local copies, waits for them, and re-layouts: 11.1 us -> 1.5 us
    mul x2 -> x0, other arithmetic: 6.77 us -> none  [finish(): (summed[0] * scale_root + decay_coef * own_w) * own_live[:, None, None]]
    reshape x2 -> x0, local copies, waits for them, and re-layouts: 5.53 us -> none  [the longest x1 2.76 us: local(): cotangent.reshape(ntok, dblocks, block)]
  transfers between devices with their start and end apart: 7 -> 0, of which waited for: 5 -> 0; matrix products, arithmetic and copies ran while one was open for 25% -> 0% of each run, Pallas kernels for 0% -> 0%
where the time goes in v1:
time: 188 us; the launch traced here: 187 us
  Pallas kernels  178 us (95%)
  other arithmetic  5.83 us (3%)
  between operations  1.97 us (1%)
    pallas_call x1, Pallas kernels, scatter(): pl.pallas_call(functools.partial(scatter_kernel, n, nd), out_shape=(jax.S...  75.8 us
    pallas_call x1, Pallas kernels, gather(): pl.pallas_call(functools.partial(gather_kernel, n), out_shape=(full, full...  64.9 us
    pallas_call x1, Pallas kernels, compute(): pl.pallas_call(compute_kernel, out_shape=(full, full, jax.ShapeDtypeStruc...  37 us
    select_n x1, other arithmetic, finish(): jnp.where(live[:, None, None], summed * scale_root + decay_coef * own_w,...  5.82 us

profile of v1, /device:TPU:0, one launch (start us, length us, event | category | flops | bytes accessed | tf_op | source)
XLA Modules:
  0.0 187.1 jit_solution(6688961823705163788)
XLA Ops:
  0.6 64.9 %shard_map.146 = (bf16[8,192,1024]{2,1,0:T(8,128)(2,1)}, bf16[8,192,1024]{2,1,0:T(8,128)(2,1)}) custom-call(bf16[192,1024]{1,0:T(8,128)(2,1)} %x_ref.1, bf16[192,1024]{1,0:T(8,128)(2,1)} %dy_ref.1), custom_call_target="tpu_custom_call" | custom-call | tf_op jit(solution)/shard_map/pallas_call | solution.py:82
  66.9 37.0 %shard_map.147 = (bf16[8,192,1024]{2,1,0:T(8,128)(2,1)}, bf16[8,192,1024]{2,1,0:T(8,128)(2,1)}, bf16[3,96,128,128]{3,2,1,0:T(8,128)(2,1)}) custom-call(s32[96]{0:T(128)} %bitcast.16, s32[96]{0:T(128)} %bitcast.17, s32[1]{0:T(128)} %copy.18.count_ref, s32[96]{0:T(128)} %bitcast.18, s32[96]{0:T(128)} %bitcast.19, s32[1]{0:T(128)} %copy.19.dcount_ref, ...), custom_call_target="tpu_custom_call" | custom-call | tf_op jit(solution)/shard_map/pallas_call | solution.py:228
  103.8 75.8 %shard_map.148 = (bf16[192,1024]{1,0:T(8,128)(2,1)}, bf16[192,1024]{1,0:T(8,128)(2,1)}, f32[3,24,128,128]{3,2,1,0:T(8,128)}) custom-call(bf16[8,192,1024]{2,1,0:T(8,128)(2,1)} %get-tuple-element.15.op_ref, bf16[8,192,1024]{2,1,0:T(8,128)(2,1)} %get-tuple-element.16.ip_ref, bf16[3,2,2,24,128,128]{5,4,3,2,1,0:T(8,128)(2,1)} %bitcast.12), custom_call_target="tpu_custom_call" | custom-call | tf_op jit(solution)/shard_map/pallas_call | solution.py:367
  179.7 0.0 copy-start.1
  179.7 0.0 copy-start
  179.7 5.8 %add_select_fusion.1 = (f32[1,24,128,128]{3,2,1,0:T(8,128)}, f32[1,24,128,128]{3,2,1,0:T(8,128)}, f32[1,24,128,128]{3,2,1,0:T(8,128)}) fusion(f32[3,24,128,128]{3,2,1,0:T(8,128)} %get-tuple-element.20, bf16[1,96,128,128]{3,2,1,0:T(8,128)(2,1)} %param.14, s32[]{:T(128)S(6)} %select_n.18, pred[24]{0:T(512)(128)(4,1)S(1)} %get-tuple-element.25, ...), kind=kLoop, calls=%fused_computation.1 | loop fusion | flops 5898240 | bytes 11796532 | tf_op jit(solution)/shard_map/jit(_where)/select_n | solution.py:398
  185.6 0.0 copy-done.1
  185.6 0.7 copy.20
  186.3 0.0 copy-done
  186.3 0.7 copy.21
  (1 shorter events, 0.0 us)
Async XLA Ops:
  179.7 5.8 %copy-start.1 = (bf16[192,1024]{1,0:T(8,128)(2,1)S(1)}, bf16[192,1024]{1,0:T(8,128)(2,1)}, u32[]{:S(2)}) copy-start(bf16[192,1024]{1,0:T(8,128)(2,1)} %get-tuple-element.31) | copy-start | bytes 1179652
  179.7 6.6 %copy-start = (bf16[192,1024]{1,0:T(8,128)(2,1)S(1)}, bf16[192,1024]{1,0:T(8,128)(2,1)}, u32[]{:S(2)}) copy-start(bf16[192,1024]{1,0:T(8,128)(2,1)} %get-tuple-element.32) | copy-start | bytes 1179652

commit v2 on v0

v2 whole, which is shorter than its diff:
```python
import functools
import math

import jax
import jax.numpy as jnp
from jax import lax
from jax.experimental import pallas as pl
from jax.experimental.pallas import tpu as pltpu
from jax.sharding import PartitionSpec as P

HID_DEV = 896
MESH = pl.DeviceIdType.MESH
F32 = jnp.float32
BF16 = jnp.bfloat16

decay_coef = 8.0


def ring_position(index, n):
    half, odd = index // 2, index % 2
    return (1 - odd) * half + odd * (n - 1 - half)


def ring_device(position, n):
    late = position // (n // 2)
    return (1 - late) * (2 * position) + late * (2 * (n - 1 - position) + 1)


def dot(left, right, contract):
    return lax.dot_general(left, right, (contract, ((), ())), preferred_element_type=F32)


def layer_kernel(
    n, nd, gtab_ref, dtab_ref, rows_ref, cols_ref, drows_ref, dcols_ref,
    x_ref, dy_ref, wg_ref, wu_ref, wd_ref,
    out_ref, in_ref, sum_ref,
    xs, dys, wgs, wus, wds, gu_acc, dh_acc, hid, dgu, hid_tiles, dgu_tiles, first, own, ring, grad, pair, far,
    own_sem, w_sem, ag_send, ag_recv, ring_send, ring_recv, pair_send, pair_recv, far_send, far_recv,
):
    blk = wg_ref.shape[-1]
    ntok, width = x_ref.shape
    per = width // blk
    hblocks = gu_acc.shape[0]
    half = ntok // 2
    me = lax.axis_index("mp")
    pos = ring_position(me, n)
    target = [ring_device((pos + 1) % n, n), ring_device((pos + n - 1) % n, n)]
    dp = lax.axis_index("dp")
    ny = nd // 2
    y, core = dp // 2, dp % 2
    partner = 2 * y + (1 - core)
    ahead = 2 * ((y + 1) % ny) + core
    behind = 2 * ((y + ny - 1) % ny) + core
    started = []

    loads = [
        pltpu.make_async_copy(w, held.at[pl.ds(1, w.shape[0])], w_sem.at[k])
        for k, (w, held) in enumerate(((wg_ref, wgs), (wu_ref, wus), (wd_ref, wds)))
    ]
    full = (xs, dys)
    owns = [
        pltpu.make_async_copy(
            shard.at[:, pl.ds(f * blk, blk)], full[a].at[me * per + f], own_sem.at[a, f]
        )
        for f in range(per)
        for a, shard in enumerate((x_ref, dy_ref))
    ]
    for copy in owns + loads:
        copy.start()

    barrier = pltpu.get_barrier_semaphore()
    greet = [{"mp": target[0]}, {"mp": target[1]}, {"dp": partner}, {"dp": ahead}]
    if ny > 2:
        greet.append({"dp": behind})
    for device in greet:
        pl.semaphore_signal(barrier, inc=1, device_id=device, device_id_type=MESH)
    pl.semaphore_wait(barrier, len(greet))

    def remote(src, dst, send, recv, device):
        copy = pltpu.make_async_remote_copy(
            src_ref=src, dst_ref=dst, send_sem=send, recv_sem=recv,
            device_id=device, device_id_type=MESH,
        )
        copy.start()
        started.append(copy)
        return copy

    def owner(a, s):
        return ring_device((pos + (n - s if a == 0 else s)) % n, n)

    def gather_hop(a, s, h):
        blocks = pl.ds(owner(a, s) * per + h * (per // 2), per // 2)
        return remote(
            full[a].at[blocks], full[a].at[blocks],
            ag_send.at[a, s, h], ag_recv.at[a, s, h], {"mp": target[a]},
        )

    def features(a, o):
        return jnp.concatenate([full[a][o * per + f] for f in range(per)], axis=1)

    def gate_up(o):
        def body(h, carry):
            tabs = [gtab_ref[(o * per + f) * hblocks + h] for f in range(per)]
            rhs = jnp.concatenate(
                [jnp.concatenate([wgs[t], wus[t]], axis=1) for t in tabs], axis=0
            )
            gu_acc[h] += dot(features(0, o), rhs, ((1,), (0,)))
            return carry

        lax.fori_loop(0, hblocks, body, 0)

    def hidden_back(o):
        def body(h, carry):
            tabs = [dtab_ref[(o * per + f) * hblocks + h] for f in range(per)]
            rhs = jnp.concatenate([wds[t] for t in tabs], axis=1)
            dh_acc[h] += dot(features(1, o), rhs, ((1,), (1,)))
            return carry

        lax.fori_loop(0, hblocks, body, 0)

    for copy in owns:
        copy.wait()
    hops = {}
    for h in range(2):
        for a in range(2):
            hops[a, h] = gather_hop(a, 0, h)
    gu_acc[...] = jnp.zeros_like(gu_acc)
    dh_acc[...] = jnp.zeros_like(dh_acc)
    for held in (wgs, wus, wds):
        held[0] = jnp.zeros((blk, blk), BF16)
    for copy in loads:
        copy.wait()
    gate_up(me)
    hidden_back(me)
    for s in range(1, n):
        for h in range(2):
            for a in range(2):
                hops[a, h].wait_recv()
                if s < n - 1:
                    hops[a, h] = gather_hop(a, s, h)
        gate_up(owner(0, s))
        hidden_back(owner(1, s))

    for h in range(hblocks):
        gate = gu_acc[h, :, :blk]
        up = gu_acc[h, :, blk:]
        dhid = dh_acc[h]
        sig = 1.0 / (1.0 + jnp.exp(-gate))
        act = gate * sig
        hidden = (act * up).astype(BF16)
        d_gate = (dhid * up * sig * (1.0 + gate * (1.0 - sig))).astype(BF16)
        d_up = (dhid * act).astype(BF16)
        hid[:, h * blk:(h + 1) * blk] = hidden
        hid_tiles[h] = hidden
        both = jnp.concatenate([d_gate, d_up], axis=1)
        dgu[:, 2 * h * blk:2 * (h + 1) * blk] = both
        dgu_tiles[h] = both

    def chunk(a, s):
        return ring_device((pos + (2 * n - 1 - s if a == 0 else 1 + s)) % n, n)

    def out_chunk(ref, o):
        def body(f, carry):
            base = (o * per + f) * hblocks
            rhs = jnp.concatenate([wds[dtab_ref[base + h]] for h in range(hblocks)], axis=0)
            lanes = pl.ds(pl.multiple_of(f * blk, blk), blk)
            ref[:, lanes] = dot(hid[...], rhs, ((1,), (0,))).astype(ref.dtype)
            return carry

        lax.fori_loop(0, per, body, 0)

    def in_chunk(ref, o):
        def body(f, carry):
            base = (o * per + f) * hblocks
            tabs = [gtab_ref[base + h] for h in range(hblocks)]
            rhs = jnp.concatenate([held[t] for t in tabs for held in (wgs, wus)], axis=1)
            lanes = pl.ds(pl.multiple_of(f * blk, blk), blk)
            ref[:, lanes] = dot(dgu[...], rhs, ((1,), (1,))).astype(ref.dtype)
            return carry

        lax.fori_loop(0, per, body, 0)

    own_chunk = (out_chunk, in_chunk)
    results = (out_ref, in_ref)

    def ring_hop(a, s, h):
        rows = pl.ds(h * half, half)
        src = first.at[a, rows] if s == 0 else ring.at[a, s - 1, rows]
        return remote(
            src, ring.at[a, s, rows], ring_send.at[a, s, h], ring_recv.at[a, s, h], {"mp": target[a]}
        )

    def ring_add(a, s, h):
        step = 32

        def body(i, carry):
            r = pl.multiple_of(h * half + i * step, step)
            total = (ring[a, s, pl.ds(r, step), :].astype(F32) + own[a, pl.ds(r, step), :]).astype(BF16)
            if s < n - 2:
                ring[a, s, pl.ds(r, step), :] = total
            else:
                results[a][pl.ds(r, step), :] = total
            return carry

        lax.fori_loop(0, half // step, body, 0)

    def ring_step(s):
        for h in range(2):
            for a in range(2):
                hops[a, h].wait_recv()
                ring_add(a, s, h)
                if s < n - 2:
                    hops[a, h] = ring_hop(a, s + 1, h)
        if s < n - 2:
            for a in range(2):
                own_chunk[a](own.at[a], chunk(a, s + 2))

    share = grad.shape[3]

    def group(t):
        return (y + 2 * ny - 1 - t) % ny

    def slot_grads(t, c):
        g = group(t)
        base = (2 * g + c) * share
        unit = 4

        def body(i, carry):
            for j in range(unit):
                e = i * unit + j
                s = base + e
                down = dot(hid_tiles[drows_ref[s]], dys[dcols_ref[s]], ((0,), (0,)))
                both = dot(xs[rows_ref[s]], dgu_tiles[cols_ref[s]], ((0,), (0,)))
                grad[0, g, c, e] = both[:, :blk].astype(BF16)
                grad[1, g, c, e] = both[:, blk:].astype(BF16)
                grad[2, g, c, e] = down.astype(BF16)
            return carry

        lax.fori_loop(0, share // unit, body, 0)

    pairs = {}
    fars = {}

    def give(t):
        slot_grads(t, 1 - core)
        g = group(t)
        for k in range(3):
            pairs[k, t] = remote(
                grad.at[k, g, 1 - core], pair.at[k, g],
                pair_send.at[k, t], pair_recv.at[k, t], {"dp": partner},
            )

    def keep(t):
        slot_grads(t, core)

    def pair_add(t):
        g = group(t)
        for k in range(3):
            pairs[k, t].wait_recv()
            if t > 0:
                fars[k, t - 1].wait_recv()

            def body(i, carry):
                total = pair[k, g, i].astype(F32) + grad[k, g, core, i].astype(F32)
                if t > 0:
                    total = total + far[k, t - 1, i].astype(F32)
                if t < ny - 1:
                    pair[k, g, i] = total.astype(BF16)
                else:
                    sum_ref[k, i] = total
                return carry

            lax.fori_loop(0, share, body, 0)
            if t < ny - 1:
                fars[k, t] = remote(
                    pair.at[k, g], far.at[k, t], far_send.at[k, t], far_recv.at[k, t], {"dp": ahead}
                )

    for a in range(2):
        own_chunk[a](first.at[a], chunk(a, 0))
        for h in range(2):
            hops[a, h] = ring_hop(a, 0, h)
    give(0)
    keep(0)
    for a in range(2):
        own_chunk[a](own.at[a], chunk(a, 1))
    tasks = [functools.partial(pair_add, 0)]
    for t in range(1, ny):
        tasks += [functools.partial(give, t), functools.partial(keep, t)]
        if t < ny - 1:
            tasks.append(functools.partial(pair_add, t))
    for s in range(n - 1):
        ring_step(s)
        if tasks:
            tasks.pop(0)()
    for task in tasks:
        task()
    pair_add(ny - 1)
    for copy in started:
        copy.wait_send()


def layer(tokens, out_grad, wg, wu, wd, gtab, dtab, rows, cols, drows, dcols, n, nd):
    ntok, width = tokens.shape
    slots, blk, _ = wg.shape
    share = slots // nd
    ny = nd // 2
    hblocks = HID_DEV // blk
    return pl.pallas_call(
        functools.partial(layer_kernel, n, nd),
        out_shape=(
            jax.ShapeDtypeStruct((ntok, width), BF16),
            jax.ShapeDtypeStruct((ntok, width), BF16),
            jax.ShapeDtypeStruct((3, share, blk, blk), F32),
        ),
        in_specs=[pl.BlockSpec(memory_space=pltpu.SMEM)] * 6
        + [pl.BlockSpec(memory_space=pl.ANY)] * 5,
        out_specs=(pl.BlockSpec(memory_space=pltpu.VMEM),) * 3,
        scratch_shapes=[
            pltpu.VMEM((n * width // blk, ntok, blk), BF16),
            pltpu.VMEM((n * width // blk, ntok, blk), BF16),
            pltpu.VMEM((slots + 1, blk, blk), BF16),
            pltpu.VMEM((slots + 1, blk, blk), BF16),
            pltpu.VMEM((slots + 1, blk, blk), BF16),
            pltpu.VMEM((hblocks, ntok, 2 * blk), F32),
            pltpu.VMEM((hblocks, ntok, blk), F32),
            pltpu.VMEM((ntok, hblocks * blk), BF16),
            pltpu.VMEM((ntok, 2 * hblocks * blk), BF16),
            pltpu.VMEM((hblocks, ntok, blk), BF16),
            pltpu.VMEM((hblocks, ntok, 2 * blk), BF16),
            pltpu.VMEM((2, ntok, width), BF16),
            pltpu.VMEM((2, ntok, width), F32),
            pltpu.VMEM((2, n - 1, ntok, width), BF16),
            pltpu.VMEM((3, ny, 2, share, blk, blk), BF16),
            pltpu.VMEM((3, ny, share, blk, blk), BF16),
            pltpu.VMEM((3, max(ny - 1, 1), share, blk, blk), BF16),
            pltpu.SemaphoreType.DMA((2, width // blk)),
            pltpu.SemaphoreType.DMA((3,)),
            pltpu.SemaphoreType.DMA((2, n - 1, 2)),
            pltpu.SemaphoreType.DMA((2, n - 1, 2)),
            pltpu.SemaphoreType.DMA((2, n - 1, 2)),
            pltpu.SemaphoreType.DMA((2, n - 1, 2)),
            pltpu.SemaphoreType.DMA((3, ny)),
            pltpu.SemaphoreType.DMA((3, ny)),
            pltpu.SemaphoreType.DMA((3, ny)),
            pltpu.SemaphoreType.DMA((3, ny)),
        ],
        compiler_params=pltpu.CompilerParams(
            collective_id=0, has_side_effects=True, vmem_limit_bytes=58 << 20
        ),
    )(gtab, dtab, rows, cols, drows, dcols, tokens, out_grad, wg, wu, wd)


def slot_table(features, hidden, count, dblocks, hblocks):
    slot = jnp.arange(features.shape[0])
    key = jnp.where(slot < count[0], features * hblocks + hidden, -1)
    hit = key[None, :] == jnp.arange(dblocks * hblocks)[:, None]
    return jnp.sum(jnp.where(hit, slot[None, :] + 1, 0), axis=1).astype(jnp.int32)


def finish(summed, weights, count, scale_root):
    share = summed.shape[0]
    start = lax.axis_index("dp") * share
    own_w = lax.dynamic_slice_in_dim(weights, start, share, 0).astype(F32)
    live = start + jnp.arange(share) < count[0]
    return jnp.where(live[:, None, None], summed * scale_root + decay_coef * own_w, 0.0)[None]


def local(
    tokens, out_grad, w_gate, w_up, w_down, gu_rows, gu_cols, gu_count, dn_rows, dn_cols, dn_count
):
    n = lax.axis_size("mp")
    nd = lax.axis_size("dp")
    wg, wu, wd = w_gate[0], w_up[0], w_down[0]
    scale_root = 1.0 / math.sqrt(tokens.shape[0] * nd)
    blk = wg.shape[-1]
    dblocks = tokens.shape[1] * n // blk
    hblocks = HID_DEV // blk
    gtab = slot_table(gu_rows[0], gu_cols[0], gu_count, dblocks, hblocks)
    dtab = slot_table(dn_cols[0], dn_rows[0], dn_count, dblocks, hblocks)
    ffn_out, input_grad, summed = layer(
        tokens, out_grad, wg, wu, wd, gtab, dtab,
        gu_rows[0], gu_cols[0], dn_rows[0], dn_cols[0], n, nd,
    )
    gate_step = finish(summed[0], wg, gu_count, scale_root)
    up_step = finish(summed[1], wu, gu_count, scale_root)
    down_step = finish(summed[2], wd, dn_count, scale_root)
    return (ffn_out, input_grad, gate_step, up_step, down_step)


def solution(mesh):
    in_specs = (
        P("dp", "mp"),
        P("dp", "mp"),
        P("mp", None, None, None),
        P("mp", None, None, None),
        P("mp", None, None, None),
        P("mp", None),
        P("mp", None),
        P("mp"),
        P("mp", None),
        P("mp", None),
        P("mp"),
    )
    out_specs = (
        P("dp", "mp"),
        P("dp", "mp"),
        P("mp", "dp", None, None),
        P("mp", "dp", None, None),
        P("mp", "dp", None, None),
    )
    return jax.shard_map(local, mesh=mesh, in_specs=in_specs, out_specs=out_specs, check_vma=False)
```

time: 464 us -> 158 us (0.34)
  waiting for transfers between devices: 285 us -> 0 us
  Pallas kernels: 0 us -> 147 us
  matrix products: 114 us -> 0 us
  local copies, waits for them, and re-layouts: 34.2 us -> 1.5 us
  between operations: 15.8 us -> 1.97 us
    reduce_scatter x5 -> x0, waiting for transfers between devices: 192 us -> none  [the longest x1 78.6 us: local(): lax.psum_scatter(out_part.astype(jnp.bfloat16), 'mp', scatter_dimension=1...]
    pallas_call x0 -> x1, Pallas kernels: none -> 147 us  [layer(): pl.pallas_call(functools.partial(layer_kernel, n, nd), out_shape=(jax.Sha...]
    dot_general x14 -> x0, matrix products: 114 us -> none  [the longest x5 60 us: collect(): jnp.einsum('tsn,sc->tcn', tiles, table, precision=lax.Precision.HIGH, pre...]
    all_gather x2 -> x0, waiting for transfers between devices: 92.1 us -> none  [the longest x1 60 us: local(): features = lax.all_gather(tokens, 'mp', axis=1, tiled=True)]
    gather x5 -> x0, local copies, waits for them, and re-layouts: 17.4 us -> none  [the longest x1 3.54 us: local(): h_tiles = jnp.take(hidden, dn_rows[0], axis=1)]
    unnamed x22 -> x6, local copies, waits for them, and re-layouts: 11.1 us -> 1.5 us
    mul x2 -> x0, other arithmetic: 6.77 us -> none  [finish(): (summed[0] * scale_root + decay_coef * own_w) * own_live[:, None, None]]
    reshape x2 -> x0, local copies, waits for them, and re-layouts: 5.53 us -> none  [the longest x1 2.76 us: local(): cotangent.reshape(ntok, dblocks, block)]
  transfers between devices with their start and end apart: 7 -> 0, of which waited for: 5 -> 0; matrix products, arithmetic and copies ran while one was open for 25% -> 0% of each run, Pallas kernels for 0% -> 0%
where the time goes in v2:
time: 158 us; the launch traced here: 157 us
  Pallas kernels  147 us (93%)
  other arithmetic  7.26 us (5%)
  between operations  1.97 us (1%)
    pallas_call x1, Pallas kernels, layer(): pl.pallas_call(functools.partial(layer_kernel, n, nd), out_shape=(jax.Sha...  147 us
    select_n x1, other arithmetic, finish(): jnp.where(live[:, None, None], summed * scale_root + decay_coef * own_w,...  5.82 us

profile of v2, /device:TPU:0, one launch (start us, length us, event | category | flops | bytes accessed | tf_op | source)
XLA Modules:
  0.0 157.3 jit_solution(17277042474224304309)
XLA Ops:
  2.0 0.7 fusion
  2.7 0.7 select_reduce_fusion
  3.4 146.6 %shard_map.146 = (bf16[192,1024]{1,0:T(8,128)(2,1)}, bf16[192,1024]{1,0:T(8,128)(2,1)}, f32[3,24,128,128]{3,2,1,0:T(8,128)}) custom-call(s32[448]{0:T(512)} %get-tuple-element.12.gtab_ref, s32[448]{0:T(512)} %get-tuple-element.11.dtab_ref, s32[96]{0:T(128)} %bitcast.21, s32[96]{0:T(128)} %bitcast.20, s32[96]{0:T(128)} %bitcast.22, s32[96]{0:T(128)} %bitcast.23, ...), custom_call_target="tpu_custom_call" | custom-call | tf_op jit(solution)/shard_map/pallas_call | solution.py:309
  150.0 0.0 copy-start.1
  150.0 0.0 copy-start
  150.0 5.8 %add_select_fusion.1 = (f32[1,24,128,128]{3,2,1,0:T(8,128)}, f32[1,24,128,128]{3,2,1,0:T(8,128)}, f32[1,24,128,128]{3,2,1,0:T(8,128)}) fusion(f32[3,24,128,128]{3,2,1,0:T(8,128)} %get-tuple-element.10, bf16[1,96,128,128]{3,2,1,0:T(8,128)(2,1)} %param.14, s32[]{:T(128)S(6)} %select_n.38, pred[24]{0:T(512)(128)(4,1)S(1)} %get-tuple-element.19, ...), kind=kLoop, calls=%fused_computation.1 | loop fusion | flops 5898240 | bytes 11796532 | tf_op jit(solution)/shard_map/jit(_where)/select_n | solution.py:366
  155.8 0.0 copy-done.1
  155.8 0.7 copy.20
  156.6 0.0 copy-done
  156.6 0.7 copy.21
  (2 shorter events, 0.0 us)
Async XLA Ops:
  150.0 5.8 %copy-start.1 = (bf16[192,1024]{1,0:T(8,128)(2,1)S(1)}, bf16[192,1024]{1,0:T(8,128)(2,1)}, u32[]{:S(2)}) copy-start(bf16[192,1024]{1,0:T(8,128)(2,1)} %get-tuple-element.25) | copy-start | bytes 1179652
  150.0 6.6 %copy-start = (bf16[192,1024]{1,0:T(8,128)(2,1)S(1)}, bf16[192,1024]{1,0:T(8,128)(2,1)}, u32[]{:S(2)}) copy-start(bf16[192,1024]{1,0:T(8,128)(2,1)} %get-tuple-element.26) | copy-start | bytes 1179652

commit v3 on v2

--- a/solution.py
+++ b/solution.py
@@ -161,24 +161,42 @@
 
     def out_chunk(ref, o):
         def body(f, carry):
-            base = (o * per + f) * hblocks
-            rhs = jnp.concatenate([wds[dtab_ref[base + h]] for h in range(hblocks)], axis=0)
-            lanes = pl.ds(pl.multiple_of(f * blk, blk), blk)
+            base = (o * per + 2 * f) * hblocks
+            rhs = jnp.concatenate(
+                [
+                    jnp.concatenate([wds[dtab_ref[base + j * hblocks + h]] for j in range(2)], axis=1)
+                    for h in range(hblocks)
+                ],
+                axis=0,
+            )
+            lanes = pl.ds(pl.multiple_of(f * 2 * blk, 2 * blk), 2 * blk)
             ref[:, lanes] = dot(hid[...], rhs, ((1,), (0,))).astype(ref.dtype)
             return carry
 
-        lax.fori_loop(0, per, body, 0)
+        lax.fori_loop(0, per // 2, body, 0)
 
     def in_chunk(ref, o):
         def body(f, carry):
-            base = (o * per + f) * hblocks
-            tabs = [gtab_ref[base + h] for h in range(hblocks)]
-            rhs = jnp.concatenate([held[t] for t in tabs for held in (wgs, wus)], axis=1)
-            lanes = pl.ds(pl.multiple_of(f * blk, blk), blk)
+            base = (o * per + 2 * f) * hblocks
+            rhs = jnp.concatenate(
+                [
+                    jnp.concatenate(
+                        [
+                            held[t]
+                            for t in [gtab_ref[base + j * hblocks + h] for h in range(hblocks)]
+                            for held in (wgs, wus)
+                        ],
+                        axis=1,
+                    )
+                    for j in range(2)
+                ],
+                axis=0,
+            )
+            lanes = pl.ds(pl.multiple_of(f * 2 * blk, 2 * blk), 2 * blk)
             ref[:, lanes] = dot(dgu[...], rhs, ((1,), (1,))).astype(ref.dtype)
             return carry
 
-        lax.fori_loop(0, per, body, 0)
+        lax.fori_loop(0, per // 2, body, 0)
 
     own_chunk = (out_chunk, in_chunk)
     results = (out_ref, in_ref)
@@ -284,7 +302,8 @@
     keep(0)
     for a in range(2):
         own_chunk[a](own.at[a], chunk(a, 1))
-    tasks = [functools.partial(pair_add, 0)]
+    pair_add(0)
+    tasks = []
     for t in range(1, ny):
         tasks += [functools.partial(give, t), functools.partial(keep, t)]
         if t < ny - 1:

time: 158 us -> 150 us (0.949)
  Pallas kernels: 147 us -> 139 us
    pallas_call x1, Pallas kernels: 147 us -> 139 us  [layer(): pl.pallas_call(functools.partial(layer_kernel, n, nd), out_shape=(jax.Sha...]
where the time goes in v3:
time: 150 us
  Pallas kernels  139 us (93%)
  other arithmetic  7.26 us (5%)
  between operations  1.97 us (1%)
  local copies, waits for them, and re-layouts  1.5 us (1%)
    pallas_call x1, Pallas kernels, layer(): pl.pallas_call(functools.partial(layer_kernel, n, nd), out_shape=(jax.Sha...  139 us
    select_n x1, other arithmetic, finish(): jnp.where(live[:, None, None], summed * scale_root + decay_coef * own_w,...  5.82 us

profile of v3, /device:TPU:0, one launch (start us, length us, event | category | flops | bytes accessed | tf_op | source)
XLA Modules:
  0.0 150.1 jit_solution(10266132682679069730)
XLA Ops:
  2.0 0.7 fusion
  2.7 0.7 select_reduce_fusion
  3.4 139.3 %shard_map.146 = (bf16[192,1024]{1,0:T(8,128)(2,1)}, bf16[192,1024]{1,0:T(8,128)(2,1)}, f32[3,24,128,128]{3,2,1,0:T(8,128)}) custom-call(s32[448]{0:T(512)} %get-tuple-element.12.gtab_ref, s32[448]{0:T(512)} %get-tuple-element.11.dtab_ref, s32[96]{0:T(128)} %bitcast.21, s32[96]{0:T(128)} %bitcast.20, s32[96]{0:T(128)} %bitcast.22, s32[96]{0:T(128)} %bitcast.23, ...), custom_call_target="tpu_custom_call" | custom-call | tf_op jit(solution)/shard_map/pallas_call | solution.py:328
  142.7 0.0 copy-start.1
  142.7 0.0 copy-start
  142.7 5.8 %add_select_fusion.1 = (f32[1,24,128,128]{3,2,1,0:T(8,128)}, f32[1,24,128,128]{3,2,1,0:T(8,128)}, f32[1,24,128,128]{3,2,1,0:T(8,128)}) fusion(f32[3,24,128,128]{3,2,1,0:T(8,128)} %get-tuple-element.10, bf16[1,96,128,128]{3,2,1,0:T(8,128)(2,1)} %param.14, s32[]{:T(128)S(6)} %select_n.38, pred[24]{0:T(512)(128)(4,1)S(1)} %get-tuple-element.19, ...), kind=kLoop, calls=%fused_computation.1 | loop fusion | flops 5898240 | bytes 11796532 | tf_op jit(solution)/shard_map/jit(_where)/select_n | solution.py:385
  148.6 0.0 copy-done.1
  148.6 0.7 copy.20
  149.3 0.0 copy-done
  149.3 0.7 copy.21
  (2 shorter events, 0.0 us)
Async XLA Ops:
  142.7 5.8 %copy-start.1 = (bf16[192,1024]{1,0:T(8,128)(2,1)S(1)}, bf16[192,1024]{1,0:T(8,128)(2,1)}, u32[]{:S(2)}) copy-start(bf16[192,1024]{1,0:T(8,128)(2,1)} %get-tuple-element.25) | copy-start | bytes 1179652
  142.7 6.6 %copy-start = (bf16[192,1024]{1,0:T(8,128)(2,1)S(1)}, bf16[192,1024]{1,0:T(8,128)(2,1)}, u32[]{:S(2)}) copy-start(bf16[192,1024]{1,0:T(8,128)(2,1)} %get-tuple-element.26) | copy-start | bytes 1179652
